TPU v7x, 32 devices: a whole 2x2x4 slice. The times are simulated.
32 devices in a mesh: gx: 4 (over z), gy: 4 (over x, core), gz: 2 (over y).
Axes of the slice: x: 2, y: 2, z: 4, core: 2. Of those that a mesh axis runs over, the one named last changes fastest.
Arguments:
- hidden: bfloat16 [12288, 4608], P(('gx', 'gy', 'gz')), may hold values from -6 to 6
- out_grad: bfloat16 [12288, 1152], P(('gx', 'gy', 'gz')), may hold values from -6 to 6
- down_weight: bfloat16 [4608, 1152], replicated, may hold values from -0.1875 to 0.1875
Outputs:
- weight_grad: float32 [4608, 1152], P(('gx', 'gy', 'gz'))
- hidden_grad: bfloat16 [12288, 4608], P(('gx', 'gy', 'gz'))
All inputs are finite; a program needn't handle non-finite values.
Results may differ from a plain program's by a relative error of at most 0.001.
Values may be sent and summed in bfloat16 or wider, within the bound.
A program may use at most 128 MiB of HBM per device.

v0:
```python
import jax
import jax.numpy as jnp
from jax import lax
from jax.sharding import PartitionSpec as P


def body(hidden, out_grad, down_weight):
    size_gx = lax.axis_size("gx")
    size_gy = lax.axis_size("gy")
    size_gz = lax.axis_size("gz")
    total_tokens = hidden.shape[0] * size_gx * size_gy * size_gz
    factor = 1.0 / jnp.sqrt(jnp.float32(total_tokens))
    features = down_weight.shape[0]
    groups = size_gx * size_gy
    own_rows = features // size_gz
    blocked = hidden.reshape(hidden.shape[0], groups, features // groups)
    traded = lax.all_to_all(blocked, "gz", split_axis=2, concat_axis=0, tiled=True)
    local_hidden = traded.reshape(traded.shape[0], own_rows)
    group_grad = lax.all_gather(out_grad, "gz", axis=0, tiled=True)
    summed = lax.psum_scatter(
        lax.dot_general(
            local_hidden, group_grad, (((0,), (0,)), ((), ())), preferred_element_type=jnp.float32
        ),
        ("gx", "gy"),
        scatter_dimension=0,
        tiled=True,
    )
    weight_grad = summed * factor
    product = lax.dot_general(
        out_grad, down_weight, (((1,), (1,)), ((), ())), preferred_element_type=jnp.float32
    )
    hidden_grad = product.astype(jnp.bfloat16)
    return (weight_grad, hidden_grad)


def solution(mesh):
    in_specs = (P(("gx", "gy", "gz"), None), P(("gx", "gy", "gz"), None), P())
    out_specs = (P(("gx", "gy", "gz"), None), P(("gx", "gy", "gz"), None))
    return jax.shard_map(body, mesh=mesh, in_specs=in_specs, out_specs=out_specs, check_vma=False)
```

profile of v0, /device:TPU:18, one launch (start us, length us, event | category | flops | bytes accessed | tf_op | source)
XLA Modules:
  0.0 220.7 jit_solution(3199882708706474189)
XLA Ops:
  7.2 4.4 %copy.7 = bf16[384,4608]{0,1:T(8,128)(2,1)S(1)} copy(bf16[384,4608]{1,0:T(8,128)(2,1)} %param.3) | data formatting | bytes 7077888 | tf_op args[0]
  11.6 3.1 %copy.8 = bf16[384,16,288]{0,1,2:T(8,128)(2,1)} copy(bf16[384,16,288]{0,2,1:T(8,128)(2,1)S(1)} %bitcast.15) | data formatting | bytes 7077888 | tf_op jit(solution)/shard_map/reshape | solution.py:16
  14.6 4.0 %all-to-all-start = ((bf16[384,16,288]{0,1,2:T(8,128)(2,1)}), bf16[384,16,288]{0,1,2:T(8,128)(2,1)S(1)}, u32[]{:S(2)}, u32[]{:S(2)}) async-start(bf16[384,16,288]{0,1,2:T(8,128)(2,1)} %copy.8), calls=%async_computation | async-start | bytes 7077888 | tf_op jit(solution)/shard_map/all_to_all | solution.py:17
  18.7 0.0 all-gather.2.cloned.1.call-start
  18.7 0.7 all-gather.2.cloned.1.call-update
  19.4 0.0 reduce-scatter.2.cloned.1.call-start
  19.4 58.7 %all-to-all-done = bf16[384,16,288]{0,1,2:T(8,128)(2,1)S(1)} async-done(((bf16[384,16,288]{0,1,2:T(8,128)(2,1)}), bf16[384,16,288]{0,1,2:T(8,128)(2,1)S(1)}, u32[]{:S(2)}, u32[]{:S(2)}) %all-to-all-start) | async-done | bytes 3538976 | tf_op jit(solution)/shard_map/all_to_all | solution.py:17
  78.2 3.6 %copy.10 = bf16[2,384,16,144]{1,0,3,2:T(2,128)(2,1)S(1)} copy(bf16[2,384,16,144]{1,2,3,0:T(8,128)(2,1)S(1)} %bitcast.13) | data formatting | bytes 7077888 | tf_op jit(solution)/shard_map/all_to_all | solution.py:17
  81.8 0.6 copy.12
  82.4 0.0 all-gather.2.cloned.1.call-done
  82.4 8.8 %fusion = f32[2304,1152]{1,0:T(8,128)} fusion(bf16[768,2304]{0,1:T(8,128)(2,1)S(1)} %bitcast.16, bf16[768,1152]{1,0:T(8,128)(2,1)} %all-gather.2.cloned.1.call-done), kind=kOutput, calls=%fused_computation.2 | convolution fusion | flops 4076863488 | bytes 15925248 | tf_op jit(solution)/shard_map/dot_general | solution.py:21
  91.2 0.0 copy-start
  91.2 0.0 reduce-scatter.2.cloned.1.call-update
  91.3 1.1 copy-done
  92.4 12.5 %convolution_convert_fusion = bf16[384,4608]{1,0:T(8,128)(2,1)} fusion(bf16[384,1152]{1,0:T(8,128)(2,1)S(1)} %copy-done, bf16[4608,1152]{1,0:T(8,128)(2,1)} %param.5), kind=kOutput, calls=%fused_computation | convolution fusion | flops 4078632960 | bytes 15040512 | tf_op jit(solution)/shard_map/dot_general | solution.py:29
  105.0 106.9 %reduce-scatter.2.cloned.1.call-done = f32[144,1152]{1,0:T(8,128)} async-done(((f32[2304,1152]{1,0:T(8,128)}), f32[144,1152]{1,0:T(8,128)}) %reduce-scatter.2.cloned.1.call-update) | async-done | bytes 663568 | tf_op jit(solution)/shard_map/reduce_scatter | solution.py:20
  211.9 2.0 broadcast_multiply_fusion
Async XLA Ops:
  14.6 63.5 %all-to-all-start = ((bf16[384,16,288]{0,1,2:T(8,128)(2,1)}), bf16[384,16,288]{0,1,2:T(8,128)(2,1)S(1)}, u32[]{:S(2)}, u32[]{:S(2)}) async-start(bf16[384,16,288]{0,1,2:T(8,128)(2,1)} %copy.8), calls=%async_computation | async-start | bytes 7077888 | tf_op jit(solution)/shard_map/all_to_all | solution.py:17
  18.7 63.8 %all-gather.2.cloned.1.call-start = ((), (), s32[]{:S(2)}) async-start(), calls=%async_computation.2 | async-start | bytes 2654208 | tf_op jit(solution)/shard_map/all_gather | solution.py:19
  19.4 192.5 %reduce-scatter.2.cloned.1.call-start = ((), (), s32[]{:S(2)}) async-start(), calls=%async_computation.3 | async-start | bytes 11280384 | tf_op jit(solution)/shard_map/reduce_scatter | solution.py:20
  91.2 1.2 copy-start
Sparse Core Ops, SparseCore 0:
  21.0 49.9 all-gather.1
  91.4 120.4 reduce-scatter.1
where the time goes:
time: 223 us; the launch traced here: 221 us
  waiting for transfers between devices  166 us (74%)
  matrix products  21.3 us (10%)
  between operations  14.1 us (6%)
  local copies, waits for them, and re-layouts  12.9 us (6%)
  starting transfers between devices  4.1 us (2%)
    reduce_scatter x1, waiting for transfers between devices, body(): lax.psum_scatter(lax.dot_general(local_hidden, group_grad, (((0,), (0,)),...  107 us
    all_to_all x1, waiting for transfers between devices, body(): lax.all_to_all(blocked, 'gz', split_axis=2, concat_axis=0, tiled=True)  58.7 us
    dot_general x1, matrix products, body(): lax.dot_general(out_grad, down_weight, (((1,), (1,)), ((), ())), preferre...  12.5 us
    dot_general x1, matrix products, body(): lax.dot_general(local_hidden, group_grad, (((0,), (0,)), ((), ())), prefe...  8.8 us
    unnamed x4, local copies, waits for them, and re-layouts  6.15 us
  transfers between devices with their start and end apart: 3, of which 2 were waited for; matrix products, arithmetic and copies ran while one was open for 8% of the time, Pallas kernels for 0%

commit v1 on v0

v1 whole, which is shorter than its diff:
```python
import functools

import jax
import jax.numpy as jnp
from jax import lax
from jax.experimental import pallas as pl
from jax.experimental.pallas import tpu as pltpu
from jax.sharding import PartitionSpec as P

MESH = pl.DeviceIdType.MESH
PLACES = ((0, 0), (1, 0), (0, 1), (1, 1))


def kernel(layers, pieces, total_tokens, ht_ref, og_ref, out_ref, held, grads, sums, below, above,
           og_send, og_recv, hid_send, hid_recv, up_send, up_recv, down_send, down_recv):
    gx, gy, y = lax.axis_index("gx"), lax.axis_index("gy"), lax.axis_index("gz")
    x, core = gy // 2, gy % 2
    rows, columns = out_ref.shape
    tokens = og_ref.shape[0]
    half = tokens // 2
    last = layers - 1

    def peer(flip, place):
        px = 1 - x if place[0] else x
        py = 1 - y if place[1] else y
        pc = 1 - core if flip else core
        return px, pc, py

    def device(who):
        px, pc, py = who
        return (gx, px * 2 + pc, py)

    peers = [(flip, at) for flip in range(2) for at in range(4) if (flip, at) != (0, 0)]
    barrier = pltpu.get_barrier_semaphore()
    for flip, at in peers:
        pl.semaphore_signal(barrier, inc=1, device_id=device(peer(flip, PLACES[at])), device_id_type=MESH)

    @pl.when(gx > 0)
    def _():
        pl.semaphore_signal(barrier, inc=1, device_id=(gx - 1, gy, y), device_id_type=MESH)

    @pl.when(gx < last)
    def _():
        pl.semaphore_signal(barrier, inc=1, device_id=(gx + 1, gy, y), device_id_type=MESH)

    inner = jnp.logical_and(gx > 0, gx < last)

    @pl.when(inner)
    def _():
        pl.semaphore_wait(barrier, len(peers) + 2)

    @pl.when(jnp.logical_not(inner))
    def _():
        pl.semaphore_wait(barrier, len(peers) + 1)

    def send(src, dst, send_sem, recv_sem, who):
        return pltpu.make_async_remote_copy(
            src_ref=src, dst_ref=dst, send_sem=send_sem, recv_sem=recv_sem,
            device_id=who, device_id_type=MESH)

    first, second = pl.ds(0, half), pl.ds(half, half)
    across_x, across_y = device(peer(0, PLACES[1])), device(peer(0, PLACES[2]))
    sibling = device(peer(1, PLACES[0]))

    def og_copy(index, src, dst, who):
        return send(src, dst, og_send.at[index], og_recv.at[index], who)

    to_x = og_copy(0, og_ref, grads.at[0, 1], across_x)
    to_y = og_copy(1, og_ref, grads.at[0, 2], across_y)
    diag_y = og_copy(2, grads.at[0, 1, first], grads.at[0, 3, first], across_y)
    diag_x = og_copy(3, grads.at[0, 2, second], grads.at[0, 3, second], across_x)
    to_sib = [
        og_copy(4, og_ref, grads.at[1, 0], sibling),
        og_copy(5, grads.at[0, 1], grads.at[1, 1], sibling),
        og_copy(6, grads.at[0, 2], grads.at[1, 2], sibling),
        og_copy(7, grads.at[0, 3, first], grads.at[1, 3, first], sibling),
        og_copy(8, grads.at[0, 3, second], grads.at[1, 3, second], sibling),
    ]

    def hid_copy(zb, flip, at):
        who = peer(flip, PLACES[at])
        return send(ht_ref.at[zb, who[0], who[1], who[2]], held.at[zb, flip, at],
                    hid_send.at[zb, flip, at], hid_recv.at[zb, flip, at], device(who))

    def send_hidden(zb):
        for at in (3, 1, 2, 0):
            for flip in range(2):
                if (flip, at) != (0, 0):
                    hid_copy(zb, flip, at).start()

    order = []
    for step in range((layers + 1) // 2):
        order += [last - step] if last - step == step else [last - step, step]

    to_x.start()
    to_y.start()
    to_sib[0].start()
    send_hidden(order[0])
    to_x.wait_recv()
    diag_y.start()
    to_sib[1].start()
    to_y.wait_recv()
    diag_x.start()
    to_sib[2].start()
    for zb in order[1:]:
        send_hidden(zb)
    diag_y.wait_recv()
    to_sib[3].start()
    diag_x.wait_recv()
    to_sib[4].start()
    for copy in to_sib:
        copy.wait_recv()

    width = columns // 3 if columns % 384 == 0 else columns
    piece = rows // pieces

    def up_copy(zb, k):
        part = pl.ds(k * piece, piece)
        return send(sums.at[zb, part], below.at[zb, part], up_send.at[zb, k], up_recv.at[zb, k],
                    (gx + 1, gy, y))

    def down_copy(zb, k):
        part = pl.ds(k * piece, piece)
        return send(sums.at[zb, part], above.at[zb, part], down_send.at[zb, k], down_recv.at[zb, k],
                    (gx - 1, gy, y))

    def compute(zb):
        for flip, at in peers:
            hid_copy(zb, flip, at).wait_recv()

        @pl.loop(0, columns // width)
        def _(n):
            part = pl.ds(pl.multiple_of(n * width, width), width)
            total = jnp.dot(ht_ref[zb, x, core, y], og_ref[:, part], preferred_element_type=jnp.float32)
            for flip, at in peers:
                total += jnp.dot(held[zb, flip, at], grads[flip, at, :, part],
                                 preferred_element_type=jnp.float32)
            sums[zb, :, part] = total

        if zb > 0:
            @pl.when(gx == 0)
            def _():
                for k in range(pieces):
                    up_copy(zb, k).start()
        if zb < last:
            @pl.when(gx == last)
            def _():
                for k in range(pieces):
                    down_copy(zb, k).start()

    factor = 1.0 / jnp.sqrt(jnp.float32(total_tokens))

    def relay(zb):
        if zb > 1:
            @pl.when(jnp.logical_and(gx > 0, gx < zb))
            def _():
                for k in range(pieces):
                    part = pl.ds(k * piece, piece)
                    up_copy(zb, k).wait_recv()
                    sums[zb, part] += below[zb, part]
                    up_copy(zb, k).start()
        if zb < last - 1:
            @pl.when(jnp.logical_and(gx > zb, gx < last))
            def _():
                for k in range(pieces):
                    part = pl.ds(k * piece, piece)
                    down_copy(zb, k).wait_recv()
                    sums[zb, part] += above[zb, part]
                    down_copy(zb, k).start()

    def finish(zb):
        @pl.when(gx == zb)
        def _():
            for k in range(pieces):
                part = pl.ds(k * piece, piece)
                total = sums[zb, part]
                if zb > 0:
                    up_copy(zb, k).wait_recv()
                    total += below[zb, part]
                if zb < last:
                    down_copy(zb, k).wait_recv()
                    total += above[zb, part]
                out_ref[part, :] = total * factor

    for step, zb in enumerate(order):
        compute(zb)
        if step > 0:
            relay(order[step - 1])
    relay(order[-1])
    for zb in order:
        finish(zb)

    for copy in [to_x, to_y, diag_y, diag_x] + to_sib:
        copy.wait_send()
    for zb in order:
        for flip, at in peers:
            hid_copy(zb, flip, at).wait_send()
        if zb > 0:
            @pl.when(gx < zb)
            def _():
                for k in range(pieces):
                    up_copy(zb, k).wait_send()
        if zb < last:
            @pl.when(gx > zb)
            def _():
                for k in range(pieces):
                    down_copy(zb, k).wait_send()


def body(hidden, out_grad, down_weight):
    layers = lax.axis_size("gx")
    devices = layers * lax.axis_size("gy") * lax.axis_size("gz")
    tokens, features = hidden.shape
    columns = out_grad.shape[1]
    rows = features // devices
    pieces = 3 if rows % 24 == 0 else 1
    turned = hidden.T.reshape(layers, 2, 2, 2, rows, tokens)
    vmem = pl.BlockSpec(memory_space=pltpu.VMEM)
    dma = pltpu.SemaphoreType.DMA
    weight_grad = pl.pallas_call(
        functools.partial(kernel, layers, pieces, tokens * devices),
        out_shape=jax.ShapeDtypeStruct((rows, columns), jnp.float32),
        in_specs=[vmem, vmem],
        out_specs=vmem,
        scratch_shapes=[
            pltpu.VMEM((layers, 2, 4, rows, tokens), jnp.bfloat16),
            pltpu.VMEM((2, 4, tokens, columns), jnp.bfloat16),
            pltpu.VMEM((layers, rows, columns), jnp.float32),
            pltpu.VMEM((layers, rows, columns), jnp.float32),
            pltpu.VMEM((layers, rows, columns), jnp.float32),
            dma((9,)), dma((9,)),
            dma((layers, 2, 4)), dma((layers, 2, 4)),
            dma((layers, pieces)), dma((layers, pieces)),
            dma((layers, pieces)), dma((layers, pieces)),
        ],
        compiler_params=pltpu.CompilerParams(
            collective_id=0, has_side_effects=True, vmem_limit_bytes=40 * 1024 * 1024),
        name="weight_grad",
    )(turned, out_grad)
    product = lax.dot_general(
        out_grad, down_weight, (((1,), (1,)), ((), ())), preferred_element_type=jnp.float32
    )
    return (weight_grad, product.astype(jnp.bfloat16))


def solution(mesh):
    in_specs = (P(("gx", "gy", "gz"), None), P(("gx", "gy", "gz"), None), P())
    out_specs = (P(("gx", "gy", "gz"), None), P(("gx", "gy", "gz"), None))
    return jax.shard_map(body, mesh=mesh, in_specs=in_specs, out_specs=out_specs, check_vma=False)
```

time: 223 us -> 130 us (0.58)
  waiting for transfers between devices: 166 us -> 0 us
  Pallas kernels: 0 us -> 109 us
  between operations: 14.1 us -> 0.65 us
  matrix products: 21.3 us -> 12.6 us
  local copies, waits for them, and re-layouts: 12.9 us -> 6.4 us
  starting transfers between devices: 4.1 us -> 0 us
    pallas_call x0 -> x1, Pallas kernels: none -> 109 us  [body(): pl.pallas_call(functools.partial(kernel, layers, pieces, tokens * devices...]
    reduce_scatter x1 -> x0, waiting for transfers between devices: 107 us -> none  [body(): lax.psum_scatter(lax.dot_general(local_hidden, group_grad, (((0,), (0,)),...]
    all_to_all x1 -> x0, waiting for transfers between devices: 58.7 us -> none  [body(): lax.all_to_all(blocked, 'gz', split_axis=2, concat_axis=0, tiled=True)]
    dot_general x1 -> x0, matrix products: 8.8 us -> none  [body(): lax.dot_general(local_hidden, group_grad, (((0,), (0,)), ((), ())), prefe...]
    transpose x0 -> x1, local copies, waits for them, and re-layouts: none -> 4.4 us  [body(): turned = hidden.T.reshape(layers, 2, 2, 2, rows, tokens)]
    unnamed x4 -> x3, local copies, waits for them, and re-layouts: 6.15 us -> 2 us
    all_to_all x1 -> x0, starting transfers between devices: 4.02 us -> none  [body(): lax.all_to_all(blocked, 'gz', split_axis=2, concat_axis=0, tiled=True)]
    all_to_all x1 -> x0, local copies, waits for them, and re-layouts: 3.64 us -> none  [body(): lax.all_to_all(blocked, 'gz', split_axis=2, concat_axis=0, tiled=True)]
  transfers between devices with their start and end apart: 3 -> 0, of which waited for: 2 -> 0; matrix products, arithmetic and copies ran while one was open for 8% -> 0% of each run, Pallas kernels for 0% -> 0%
where the time goes in v1:
time: 130 us; the launch traced here: 129 us
  Pallas kernels  109 us (84%)
  matrix products  12.6 us (10%)
  local copies, waits for them, and re-layouts  6.4 us (5%)
    pallas_call x1, Pallas kernels, body(): pl.pallas_call(functools.partial(kernel, layers, pieces, tokens * devices...  109 us
    dot_general x1, matrix products, body(): lax.dot_general(out_grad, down_weight, (((1,), (1,)), ((), ())), preferre...  12.6 us
    transpose x1, local copies, waits for them, and re-layouts, body(): turned = hidden.T.reshape(layers, 2, 2, 2, rows, tokens)  4.4 us

profile of v1, /device:TPU:18, one launch (start us, length us, event | category | flops | bytes accessed | tf_op | source)
XLA Modules:
  0.0 129.1 jit_solution(14781961773902594434)
XLA Ops:
  0.6 4.4 %copy.5 = bf16[4608,384]{1,0:T(8,128)(2,1)S(1)} copy(bf16[4608,384]{0,1:T(8,128)(2,1)} %bitcast.5) | data formatting | bytes 7077888 | tf_op jit(solution)/shard_map/transpose | solution.py:217
  5.0 0.0 copy-start
  5.1 1.2 copy-done
  6.2 109.4 %weight_grad.1 = f32[144,1152]{1,0:T(8,128)S(1)} custom-call(bf16[4,2,2,2,144,384]{5,4,3,2,1,0:T(8,128)(2,1)S(1)} %bitcast.4, bf16[384,1152]{1,0:T(8,128)(2,1)S(1)} %copy-done), custom_call_target="tpu_custom_call" | custom-call | tf_op jit(solution)/shard_map/weight_grad/pallas_call | solution.py:220
  115.6 12.6 %convolution_convert_fusion = bf16[384,4608]{1,0:T(8,128)(2,1)} fusion(bf16[384,1152]{1,0:T(8,128)(2,1)S(1)} %copy-done, bf16[4608,1152]{1,0:T(8,128)(2,1)} %param.5), kind=kOutput, calls=%fused_computation | convolution fusion | flops 4078632960 | bytes 15040512 | tf_op jit(solution)/shard_map/dot_general | solution.py:240
  128.2 0.8 copy.7
Async XLA Ops:
  5.0 1.2 copy-start

commit v2 on v1

v2 whole, which is shorter than its diff:
```python
import functools

import jax
import jax.numpy as jnp
from jax import lax
from jax.experimental import pallas as pl
from jax.experimental.pallas import tpu as pltpu
from jax.sharding import PartitionSpec as P

MESH = pl.DeviceIdType.MESH
PLACES = ((0, 0), (1, 0), (0, 1), (1, 1))


def kernel(layers, pieces, cuts, turn, total_tokens, hid_any, og_any, weight_any, out_ref, product_ref,
           og_ref, weight, loaded, ht_ref, held, grads, sums, below, above, load_sem,
           og_send, og_recv, hid_send, hid_recv, up_send, up_recv, down_send, down_recv):
    gx, gy, y = lax.axis_index("gx"), lax.axis_index("gy"), lax.axis_index("gz")
    x, core = gy // 2, gy % 2
    rows, columns = out_ref.shape
    tokens = og_ref.shape[0]
    half = tokens // 2
    last = layers - 1

    og_load = pltpu.make_async_copy(og_any, og_ref, load_sem.at[0])
    hid_load = pltpu.make_async_copy(hid_any, loaded if turn else ht_ref, load_sem.at[1])
    weight_load = pltpu.make_async_copy(weight_any, weight, load_sem.at[2])
    og_load.start()
    hid_load.start()
    weight_load.start()

    def peer(flip, place):
        px = 1 - x if place[0] else x
        py = 1 - y if place[1] else y
        pc = 1 - core if flip else core
        return px, pc, py

    def device(who):
        px, pc, py = who
        return (gx, px * 2 + pc, py)

    peers = [(flip, at) for flip in range(2) for at in range(4) if (flip, at) != (0, 0)]
    barrier = pltpu.get_barrier_semaphore()
    for flip, at in peers:
        pl.semaphore_signal(barrier, inc=1, device_id=device(peer(flip, PLACES[at])), device_id_type=MESH)

    @pl.when(gx > 0)
    def _():
        pl.semaphore_signal(barrier, inc=1, device_id=(gx - 1, gy, y), device_id_type=MESH)

    @pl.when(gx < last)
    def _():
        pl.semaphore_signal(barrier, inc=1, device_id=(gx + 1, gy, y), device_id_type=MESH)

    inner = jnp.logical_and(gx > 0, gx < last)

    @pl.when(inner)
    def _():
        pl.semaphore_wait(barrier, len(peers) + 2)

    @pl.when(jnp.logical_not(inner))
    def _():
        pl.semaphore_wait(barrier, len(peers) + 1)

    def send(src, dst, send_sem, recv_sem, who):
        return pltpu.make_async_remote_copy(
            src_ref=src, dst_ref=dst, send_sem=send_sem, recv_sem=recv_sem,
            device_id=who, device_id_type=MESH)

    first, second = pl.ds(0, half), pl.ds(half, half)
    across_x, across_y = device(peer(0, PLACES[1])), device(peer(0, PLACES[2]))
    sibling = device(peer(1, PLACES[0]))

    def og_copies(c):
        cols = pl.ds(*cuts[c])
        mine = og_ref.at[:, cols]
        at_x, at_y = grads.at[0, 1, :, cols], grads.at[0, 2, :, cols]
        near, far = grads.at[0, 3, first, cols], grads.at[0, 3, second, cols]
        plan = (
            (mine, at_x, across_x),
            (mine, at_y, across_y),
            (grads.at[0, 1, first, cols], near, across_y),
            (grads.at[0, 2, second, cols], far, across_x),
            (mine, grads.at[1, 0, :, cols], sibling),
            (at_x, grads.at[1, 1, :, cols], sibling),
            (at_y, grads.at[1, 2, :, cols], sibling),
            (near, grads.at[1, 3, first, cols], sibling),
            (far, grads.at[1, 3, second, cols], sibling),
        )
        return [send(src, dst, og_send.at[c, i], og_recv.at[c, i], who)
                for i, (src, dst, who) in enumerate(plan)]

    def og_begin(c):
        copies = og_copies(c)
        for i in (0, 1, 4):
            copies[i].start()

    def og_pass(c):
        copies = og_copies(c)
        for got, onward in ((0, 2), (1, 3)):
            copies[got].wait_recv()
            copies[onward].start()
            copies[got + 5].start()

    def og_end(c):
        copies = og_copies(c)
        for got in (2, 3):
            copies[got].wait_recv()
            copies[got + 5].start()
        for i in range(4, 9):
            copies[i].wait_recv()

    def hid_copy(zb, flip, at):
        who = peer(flip, PLACES[at])
        return send(ht_ref.at[zb, who[0], who[1], who[2]], held.at[zb, flip, at],
                    hid_send.at[zb, flip, at], hid_recv.at[zb, flip, at], device(who))

    def send_hidden(zb):
        for at in (3, 1, 2, 0):
            for flip in range(2):
                if (flip, at) != (0, 0):
                    hid_copy(zb, flip, at).start()

    order = []
    for step in range((layers + 1) // 2):
        order += [last - step] if last - step == step else [last - step, step]

    og_load.wait()
    og_begin(0)
    hid_load.wait()
    if turn:
        group = 8 * rows

        def turned(zb):
            block = loaded[:, zb * group:(zb + 1) * group].T
            ht_ref[zb] = block.reshape(2, 2, 2, rows, tokens)
    else:
        def turned(zb):
            pass

    turned(order[0])
    send_hidden(order[0])
    weight_load.wait()
    features = weight.shape[0]
    tile = features // layers if features % (128 * layers) == 0 else features // 9

    @pl.loop(0, features // tile)
    def _(n):
        part = pl.ds(pl.multiple_of(n * tile, tile), tile)
        product_ref[:, part] = lax.dot_general(
            og_ref[...], weight[part, :], (((1,), (1,)), ((), ())),
            preferred_element_type=jnp.float32).astype(product_ref.dtype)

    for zb in order[1:]:
        turned(zb)
    og_pass(0)
    send_hidden(order[1])
    og_end(0)

    piece = rows // pieces

    def up_copy(zb, c, k):
        part = (zb, pl.ds(k * piece, piece), pl.ds(*cuts[c]))
        return send(sums.at[part], below.at[part], up_send.at[zb, c, k], up_recv.at[zb, c, k],
                    (gx + 1, gy, y))

    def down_copy(zb, c, k):
        part = (zb, pl.ds(k * piece, piece), pl.ds(*cuts[c]))
        return send(sums.at[part], above.at[part], down_send.at[zb, c, k], down_recv.at[zb, c, k],
                    (gx - 1, gy, y))

    def compute(zb, c):
        begin, size = cuts[c]
        width = cuts[-1][1]

        @pl.loop(0, size // width)
        def _(n):
            part = pl.ds(pl.multiple_of(begin + n * width, 128), width)
            total = jnp.dot(ht_ref[zb, x, core, y], og_ref[:, part], preferred_element_type=jnp.float32)
            for flip, at in peers:
                total += jnp.dot(held[zb, flip, at], grads[flip, at, :, part],
                                 preferred_element_type=jnp.float32)
            sums[zb, :, part] = total

        if zb > 0:
            @pl.when(gx == 0)
            def _():
                for k in range(pieces):
                    up_copy(zb, c, k).start()
        if zb < last:
            @pl.when(gx == last)
            def _():
                for k in range(pieces):
                    down_copy(zb, c, k).start()

    factor = 1.0 / jnp.sqrt(jnp.float32(total_tokens))

    def relay(zb, c):
        cols = pl.ds(*cuts[c])
        if zb > 1:
            @pl.when(jnp.logical_and(gx > 0, gx < zb))
            def _():
                for k in range(pieces):
                    part = pl.ds(k * piece, piece)
                    up_copy(zb, c, k).wait_recv()
                    sums[zb, part, cols] += below[zb, part, cols]
                    up_copy(zb, c, k).start()
        if zb < last - 1:
            @pl.when(jnp.logical_and(gx > zb, gx < last))
            def _():
                for k in range(pieces):
                    part = pl.ds(k * piece, piece)
                    down_copy(zb, c, k).wait_recv()
                    sums[zb, part, cols] += above[zb, part, cols]
                    down_copy(zb, c, k).start()

    def finish(zb, c):
        cols = pl.ds(*cuts[c])

        @pl.when(gx == zb)
        def _():
            for k in range(pieces):
                part = pl.ds(k * piece, piece)
                total = sums[zb, part, cols]
                if zb > 0:
                    up_copy(zb, c, k).wait_recv()
                    total += below[zb, part, cols]
                if zb < last:
                    down_copy(zb, c, k).wait_recv()
                    total += above[zb, part, cols]
                out_ref[part, cols] = total * factor

    for step, zb in enumerate(order):
        for flip, at in peers:
            hid_copy(zb, flip, at).wait_recv()
        if step + 2 < len(order):
            send_hidden(order[step + 2])
        if step == max(len(order) - 2, 0):
            for c in range(1, len(cuts)):
                og_begin(c)
        compute(zb, 0)
        if step > 0:
            relay(order[step - 1], 0)
    for c in range(1, len(cuts)):
        og_pass(c)
        og_end(c)
        for step, zb in enumerate(order):
            compute(zb, c)
            if step == 1:
                relay(order[-1], c - 1)
        for zb in order[:-1]:
            relay(zb, c)
    relay(order[-1], len(cuts) - 1)
    for c in range(len(cuts)):
        for zb in order:
            finish(zb, c)

    for c in range(len(cuts)):
        for copy in og_copies(c):
            copy.wait_send()
    for zb in order:
        for flip, at in peers:
            hid_copy(zb, flip, at).wait_send()
        for c in range(len(cuts)):
            if zb > 0:
                @pl.when(gx < zb)
                def _():
                    for k in range(pieces):
                        up_copy(zb, c, k).wait_send()
            if zb < last:
                @pl.when(gx > zb)
                def _():
                    for k in range(pieces):
                        down_copy(zb, c, k).wait_send()


def body(hidden, out_grad, down_weight):
    layers = lax.axis_size("gx")
    devices = layers * lax.axis_size("gy") * lax.axis_size("gz")
    tokens, features = hidden.shape
    columns = out_grad.shape[1]
    rows = features // devices
    pieces = 3 if rows % 24 == 0 else 1
    third = columns // 3
    cuts = ((0, 2 * third), (2 * third, third)) if columns % 384 == 0 else ((0, columns),)
    turn = rows % 16 == 0
    shape = (layers, 2, 2, 2, rows, tokens)
    source = hidden if turn else hidden.T.reshape(shape)
    vmem = pl.BlockSpec(memory_space=pltpu.VMEM)
    anywhere = pl.BlockSpec(memory_space=pl.ANY)
    dma = pltpu.SemaphoreType.DMA
    return tuple(pl.pallas_call(
        functools.partial(kernel, layers, pieces, cuts, turn, tokens * devices),
        out_shape=(
            jax.ShapeDtypeStruct((rows, columns), jnp.float32),
            jax.ShapeDtypeStruct((tokens, features), jnp.bfloat16),
        ),
        in_specs=[anywhere] * 3,
        out_specs=(vmem, vmem),
        scratch_shapes=[
            pltpu.VMEM(out_grad.shape, jnp.bfloat16),
            pltpu.VMEM(down_weight.shape, jnp.bfloat16),
            pltpu.VMEM(hidden.shape if turn else (16, 128), jnp.bfloat16),
            pltpu.VMEM(shape, jnp.bfloat16),
            pltpu.VMEM((layers, 2, 4, rows, tokens), jnp.bfloat16),
            pltpu.VMEM((2, 4, tokens, columns), jnp.bfloat16),
            pltpu.VMEM((layers, rows, columns), jnp.float32),
            pltpu.VMEM((layers, rows, columns), jnp.float32),
            pltpu.VMEM((layers, rows, columns), jnp.float32),
            dma((3,)),
            dma((len(cuts), 9)), dma((len(cuts), 9)),
            dma((layers, 2, 4)), dma((layers, 2, 4)),
            dma((layers, len(cuts), pieces)), dma((layers, len(cuts), pieces)),
            dma((layers, len(cuts), pieces)), dma((layers, len(cuts), pieces)),
        ],
        compiler_params=pltpu.CompilerParams(
            collective_id=0, has_side_effects=True, vmem_limit_bytes=58 * 1024 * 1024),
        name="weight_grad",
    )(source, out_grad, down_weight))


def solution(mesh):
    in_specs = (P(("gx", "gy", "gz"), None), P(("gx", "gy", "gz"), None), P())
    out_specs = (P(("gx", "gy", "gz"), None), P(("gx", "gy", "gz"), None))
    return jax.shard_map(body, mesh=mesh, in_specs=in_specs, out_specs=out_specs, check_vma=False)
```

time: 130 us -> 110 us (0.85)
  matrix products: 12.6 us -> 0 us
  Pallas kernels: 109 us -> 103 us
    dot_general x1 -> x0, matrix products: 12.6 us -> none  [body(): lax.dot_general(out_grad, down_weight, (((1,), (1,)), ((), ())), preferre...]
    pallas_call x1, Pallas kernels: 109 us -> 103 us  [body(): pl.pallas_call(functools.partial(kernel, layers, pieces, cuts, turn, toke...]
    transpose x1 -> x0, local copies, waits for them, and re-layouts: 4.4 us -> none  [body(): turned = hidden.T.reshape(layers, 2, 2, 2, rows, tokens)]
    unnamed x3 -> x2, local copies, waits for them, and re-layouts: 2 us -> 5.99 us
where the time goes in v2:
time: 110 us; the launch traced here: 109 us
  Pallas kernels  103 us (94%)
  local copies, waits for them, and re-layouts  5.99 us (5%)
    pallas_call x1, Pallas kernels, body(): pl.pallas_call(functools.partial(kernel, layers, pieces, cuts, turn, toke...  103 us
    unnamed x2, local copies, waits for them, and re-layouts  5.99 us

profile of v2, /device:TPU:18, one launch (start us, length us, event | category | flops | bytes accessed | tf_op | source)
XLA Modules:
  0.0 109.4 jit_solution(14417355851159679051)
XLA Ops:
  0.6 102.8 %weight_grad.1 = (f32[144,1152]{1,0:T(8,128)}, bf16[384,4608]{1,0:T(8,128)(2,1)}) custom-call(bf16[384,4608]{1,0:T(8,128)(2,1)} %hid_any.1, bf16[384,1152]{1,0:T(8,128)(2,1)} %og_any.1, bf16[4608,1152]{1,0:T(8,128)(2,1)} %weight_any.1), custom_call_target="tpu_custom_call" | custom-call | tf_op jit(solution)/shard_map/weight_grad/pallas_call | solution.py:291
  103.4 2.0 %copy.7 = f32[144,1152]{1,0:T(8,128)} copy(f32[144,1152]{1,0:T(8,128)} %get-tuple-element.4) | data formatting | bytes 1327104
  105.4 4.0 %copy.8 = bf16[384,4608]{1,0:T(8,128)(2,1)} copy(bf16[384,4608]{1,0:T(8,128)(2,1)} %get-tuple-element.5) | data formatting | bytes 7077888

commit v3 on v2

--- a/solution.py
+++ b/solution.py
@@ -138,7 +138,6 @@
             pass
 
     turned(order[0])
-    send_hidden(order[0])
     weight_load.wait()
     features = weight.shape[0]
     tile = features // layers if features % (128 * layers) == 0 else features // 9
@@ -153,6 +152,7 @@
     for zb in order[1:]:
         turned(zb)
     og_pass(0)
+    send_hidden(order[0])
     send_hidden(order[1])
     og_end(0)
 
@@ -313,7 +313,7 @@
             dma((layers, len(cuts), pieces)), dma((layers, len(cuts), pieces)),
         ],
         compiler_params=pltpu.CompilerParams(
-            collective_id=0, has_side_effects=True, vmem_limit_bytes=58 * 1024 * 1024),
+            collective_id=0, has_side_effects=True, vmem_limit_bytes=44 * 1024 * 1024),
         name="weight_grad",
     )(source, out_grad, down_weight))
 

time: 110 us -> 107 us (0.973)
  Pallas kernels: 103 us -> 100 us
    pallas_call x1, Pallas kernels: 103 us -> 100 us  [body(): pl.pallas_call(functools.partial(kernel, layers, pieces, cuts, turn, toke...]
    unnamed x2 -> x6, local copies, waits for them, and re-layouts: 5.99 us -> 5.8 us
where the time goes in v3:
time: 107 us
  Pallas kernels  100 us (93%)
  local copies, waits for them, and re-layouts  5.8 us (5%)
    pallas_call x1, Pallas kernels, body(): pl.pallas_call(functools.partial(kernel, layers, pieces, cuts, turn, toke...  100 us
    unnamed x6, local copies, waits for them, and re-layouts  5.8 us

profile of v3, /device:TPU:18, one launch (start us, length us, event | category | flops | bytes accessed | tf_op | source)
XLA Modules:
  0.0 106.9 jit_solution(7827021349359535277)
XLA Ops:
  0.6 0.0 copy-start
  0.6 2.0 %copy-done = bf16[384,4608]{1,0:T(8,128)(2,1)S(1)} copy-done((bf16[384,4608]{1,0:T(8,128)(2,1)S(1)}, bf16[384,4608]{1,0:T(8,128)(2,1)}, u32[]{:S(2)}) %copy-start) | copy-done | bytes 3538968
  2.6 0.0 copy-start.1
  2.6 1.2 %copy-done.1 = bf16[384,1152]{1,0:T(8,128)(2,1)S(1)} copy-done((bf16[384,1152]{1,0:T(8,128)(2,1)S(1)}, bf16[384,1152]{1,0:T(8,128)(2,1)}, u32[]{:S(2)}) %copy-start.1) | copy-done | bytes 884760
  3.8 100.4 %weight_grad.1 = (f32[144,1152]{1,0:T(8,128)S(1)}, bf16[384,4608]{1,0:T(8,128)(2,1)S(1)}) custom-call(bf16[384,4608]{1,0:T(8,128)(2,1)S(1)} %copy-done, bf16[384,1152]{1,0:T(8,128)(2,1)S(1)} %copy-done.1, bf16[4608,1152]{1,0:T(8,128)(2,1)} %weight_any.1), custom_call_target="tpu_custom_call" | custom-call | tf_op jit(solution)/shard_map/weight_grad/pallas_call | solution.py:291
  104.2 0.8 copy.7
  105.1 1.8 %copy.8 = bf16[384,4608]{1,0:T(8,128)(2,1)} copy(bf16[384,4608]{1,0:T(8,128)(2,1)S(1)} %get-tuple-element.5) | data formatting | bytes 7077888
Async XLA Ops:
  0.6 2.0 %copy-start = (bf16[384,4608]{1,0:T(8,128)(2,1)S(1)}, bf16[384,4608]{1,0:T(8,128)(2,1)}, u32[]{:S(2)}) copy-start(bf16[384,4608]{1,0:T(8,128)(2,1)} %hid_any.1) | copy-start | bytes 10616836
  2.6 1.2 %copy-start.1 = (bf16[384,1152]{1,0:T(8,128)(2,1)S(1)}, bf16[384,1152]{1,0:T(8,128)(2,1)}, u32[]{:S(2)}) copy-start(bf16[384,1152]{1,0:T(8,128)(2,1)} %og_any.1) | copy-start | bytes 2654212
